TPU v7x, 32 devices: a whole 2x2x4 slice. The times are simulated.
32 devices in a mesh: shard: 4 (over z), ctx: 2 (over core), tp: 4 (over y, x).
Axes of the slice: x: 2, y: 2, z: 4, core: 2. Of those that a mesh axis runs over, the one named last changes fastest.
Arguments:
- tokens: bfloat16 [8, 1024, 768], P('shard', 'ctx'), may hold values from -6 to 6
- time_embed: float32 [8, 768], P('shard'), may hold values from -3 to 3
- segments: int32 [8, 1024], P('shard'), may hold values from 0 to 3, never falling along the last dimension, each value on 1 to 800 neighbouring positions
- w_qkv: bfloat16 [768, 3, 768], P('shard', None, 'tp'), may hold values from -0.21875 to 0.21875
- w_out: bfloat16 [768, 768], P('tp', 'shard'), may hold values from -0.875 to 0.875
- w_up: bfloat16 [768, 3072], P('shard', 'tp'), may hold values from -0.21875 to 0.21875
- w_down: bfloat16 [3072, 768], P('tp', 'shard'), may hold values from -0.21875 to 0.21875
- qv_bias: float32 [2, 768], P(None, 'tp'), may hold values from -0.625 to 0.625
- up_bias: float32 [3072], P('tp'), may hold values from -1.75 to 1.75
- norm_gains: float32 [2, 768], replicated, may hold values from 0.5 to 1.5
- norm_shifts: float32 [2, 768], replicated, may hold values from -1.75 to 1.75
- branch_bias: float32 [2, 768], replicated, may hold values from -1.75 to 1.75
- out_grad: bfloat16 [8, 1024, 768], P('shard', 'ctx'), may hold values from -8 to 8
Outputs:
- layer_out: float32 [8, 1024, 768], P('shard', 'ctx')
- input_grad: float32 [8, 1024, 768], P('shard', 'ctx')
- w_qkv_grad: float32 [768, 3, 768], P('shard', None, 'tp')
- w_out_grad: float32 [768, 768], P('tp', 'shard')
- w_up_grad: float32 [768, 3072], P('shard', 'tp')
- w_down_grad: float32 [3072, 768], P('tp', 'shard')
- qv_bias_grad: float32 [2, 768], P(None, 'tp')
- up_bias_grad: float32 [3072], P('tp')
- norm_gains_grad: float32 [2, 768], replicated
- norm_shifts_grad: float32 [2, 768], replicated
- branch_bias_grad: float32 [2, 768], replicated
Inputs may be any that keep to these rules, and one draw needn't show every extreme that they name: `segments`: document numbers never fall along a sequence; each document holds 1 to 800 tokens, and one of each sequence exactly 800.
All inputs are finite; a program needn't handle non-finite values.
Results may differ from a plain program's by a relative error of at most 0.018.
Values may be sent and summed in bfloat16 or wider, within the bound.
No kernel may reach another device: no remote copies, remote signals or barrier semaphores. Data moves between devices by JAX's collectives and lax.ppermute only.
A program may use at most 128 MiB of HBM per device.

v0:
```python
import jax
import jax.numpy as jnp
from jax import lax
from jax.sharding import PartitionSpec as P

HD = 64


def layer_norm(residual, gain_vec, shift_vec):
    center = residual - jnp.mean(residual, axis=-1, keepdims=True)
    spread = jnp.mean(center * center, axis=-1, keepdims=True)
    return center * lax.rsqrt(spread + 1e-05) * gain_vec + shift_vec


def exact_gelu(values):
    return jax.nn.gelu(values, approximate=False)


def fetch_weights(w_qkv, w_out, w_up, w_down):
    return (
        lax.all_gather(w_qkv, "shard", axis=0, tiled=True),
        lax.all_gather(w_out, "shard", axis=1, tiled=True),
        lax.all_gather(w_up, "shard", axis=0, tiled=True),
        lax.all_gather(w_down, "shard", axis=1, tiled=True),
    )


def across_heads(term_rows):
    return lax.psum(term_rows, "tp")


def masked_scores(query_blk, key_blk, labels_query, labels_key):
    query_len = query_blk.shape[0]
    key_len = key_blk.shape[0]
    head_count = query_blk.shape[1] // HD
    query_heads = query_blk.reshape(query_len, head_count, HD)
    key_heads = key_blk.reshape(key_len, head_count, HD)
    scores = jnp.einsum(
        "qhe,khe->hqk", query_heads, key_heads, preferred_element_type=jnp.float32
    ) * HD ** (-0.5)
    same_doc = labels_query[:, None] == labels_key[None, :]
    return jnp.where(same_doc[None], scores, -1e30)


def attend_forward(packed):
    query_blk, key_blk, value_blk, labels_query, labels_key = packed
    query_len = query_blk.shape[0]
    key_len = key_blk.shape[0]
    head_count = query_blk.shape[1] // HD
    scores = masked_scores(query_blk, key_blk, labels_query, labels_key)
    row_max = jnp.max(scores, axis=-1, keepdims=True)
    exp_scores = jnp.exp(scores - row_max)
    row_total = jnp.sum(exp_scores, axis=-1, keepdims=True)
    attn_probs = exp_scores / row_total
    value_heads = value_blk.reshape(key_len, head_count, HD)
    heads_out = jnp.einsum(
        "hqk,khe->qhe",
        attn_probs.astype(jnp.bfloat16),
        value_heads,
        preferred_element_type=jnp.float32,
    )
    return (heads_out.reshape(query_len, head_count * HD), (row_max + jnp.log(row_total))[..., 0])


def attend_backward(packed):
    query_blk, key_blk, value_blk, labels_query, labels_key, grad_blk, log_total = packed
    query_len = query_blk.shape[0]
    key_len = key_blk.shape[0]
    head_count = query_blk.shape[1] // HD
    scores = masked_scores(query_blk, key_blk, labels_query, labels_key)
    attn_probs = jnp.exp(scores - log_total[..., None])
    query_heads = query_blk.reshape(query_len, head_count, HD)
    key_heads = key_blk.reshape(key_len, head_count, HD)
    value_heads = value_blk.reshape(key_len, head_count, HD)
    grad_heads = grad_blk.reshape(query_len, head_count, HD)
    grad_probs = jnp.einsum(
        "qhe,khe->hqk", grad_heads, value_heads, preferred_element_type=jnp.float32
    )
    inner_sum = jnp.sum(attn_probs * grad_probs, axis=-1, keepdims=True)
    grad_scores = (attn_probs * (grad_probs - inner_sum)).astype(jnp.bfloat16)
    grad_query = jnp.einsum(
        "hqk,khe->qhe", grad_scores, key_heads, preferred_element_type=jnp.float32
    ) * HD ** (-0.5)
    grad_key = jnp.einsum(
        "hqk,qhe->khe", grad_scores, query_heads, preferred_element_type=jnp.float32
    ) * HD ** (-0.5)
    grad_value = jnp.einsum(
        "hqk,qhe->khe",
        attn_probs.astype(jnp.bfloat16),
        grad_heads,
        preferred_element_type=jnp.float32,
    )
    return (
        grad_query.reshape(query_len, head_count * HD),
        grad_key.reshape(key_len, head_count * HD),
        grad_value.reshape(key_len, head_count * HD),
    )


def shards(
    tokens,
    time_embed,
    segments,
    w_qkv,
    w_out,
    w_up,
    w_down,
    qv_bias,
    up_bias,
    norm_gains,
    norm_shifts,
    branch_bias,
    out_grad,
):
    seq_count, half_len, model_width = tokens.shape
    row_count = seq_count * half_len
    ctx_index = lax.axis_index("ctx")
    labels_query = lax.dynamic_slice_in_dim(segments, ctx_index * half_len, half_len, 1)
    stream_in = (tokens.astype(jnp.float32) + time_embed[:, None, :]).reshape(
        row_count, model_width
    )
    stream_low = stream_in.astype(jnp.bfloat16)
    cotangent = out_grad.astype(jnp.float32).reshape(row_count, model_width)
    full_qkv, full_out, full_up, full_down = fetch_weights(w_qkv, w_out, w_up, w_down)
    head_cols = full_qkv.shape[2]
    product = jnp.dot(
        stream_low, full_qkv.reshape(model_width, 3 * head_cols), preferred_element_type=jnp.float32
    ).reshape(row_count, 3, head_cols)
    query_low = (
        (product[:, 0] + qv_bias[0]).astype(jnp.bfloat16).reshape(seq_count, half_len, head_cols)
    )
    key_low = product[:, 1].astype(jnp.bfloat16).reshape(seq_count, half_len, head_cols)
    value_low = (
        (product[:, 2] + qv_bias[1]).astype(jnp.bfloat16).reshape(seq_count, half_len, head_cols)
    )
    key_all, value_all = (
        lax.all_gather(key_low, "ctx", axis=1, tiled=True),
        lax.all_gather(value_low, "ctx", axis=1, tiled=True),
    )
    heads_out, log_total = lax.map(
        attend_forward, (query_low, key_all, value_all, labels_query, segments)
    )
    heads_low = heads_out.reshape(row_count, head_cols).astype(jnp.bfloat16)
    attn_part = jnp.dot(heads_low, full_out, preferred_element_type=jnp.float32)
    attn_out = across_heads(attn_part) + branch_bias[0]
    normed, first_pullback = jax.vjp(
        layer_norm, stream_in + attn_out, norm_gains[0], norm_shifts[0]
    )
    normed_low = normed.astype(jnp.bfloat16)
    pre_act = jnp.dot(normed_low, full_up, preferred_element_type=jnp.float32) + up_bias
    activated, gelu_pullback = jax.vjp(exact_gelu, pre_act)
    act_low = activated.astype(jnp.bfloat16)
    down_part = jnp.dot(act_low, full_down, preferred_element_type=jnp.float32)
    ffn_out = across_heads(down_part) + branch_bias[1]
    layer_rows, second_pullback = jax.vjp(
        layer_norm, normed + ffn_out, norm_gains[1], norm_shifts[1]
    )
    back_qkv, back_out, back_up, back_down = fetch_weights(w_qkv, w_out, w_up, w_down)
    grad_second, gain_second, shift_second = second_pullback(cotangent)
    grad_ffn_low = grad_second.astype(jnp.bfloat16)
    grad_down = jnp.einsum("tf,td->fd", act_low, grad_ffn_low, preferred_element_type=jnp.float32)
    grad_act = jnp.einsum("td,fd->tf", grad_ffn_low, back_down, preferred_element_type=jnp.float32)
    (grad_pre,) = gelu_pullback(grad_act)
    grad_pre_low = grad_pre.astype(jnp.bfloat16)
    grad_up = jnp.einsum("td,tf->df", normed_low, grad_pre_low, preferred_element_type=jnp.float32)
    up_part = jnp.einsum("tf,df->td", grad_pre_low, back_up, preferred_element_type=jnp.float32)
    grad_normed = across_heads(up_part) + grad_second
    grad_first, gain_first, shift_first = first_pullback(grad_normed)
    grad_attn_low = grad_first.astype(jnp.bfloat16)
    grad_out = jnp.einsum("th,td->hd", heads_low, grad_attn_low, preferred_element_type=jnp.float32)
    grad_heads = (
        jnp.einsum("td,hd->th", grad_attn_low, back_out, preferred_element_type=jnp.float32)
        .astype(jnp.bfloat16)
        .reshape(seq_count, half_len, head_cols)
    )
    grad_query, grad_key_all, grad_value_all = lax.map(
        attend_backward,
        (query_low, key_all, value_all, labels_query, segments, grad_heads, log_total),
    )
    grad_key, grad_value = (
        lax.psum_scatter(
            grad_key_all.astype(jnp.bfloat16), "ctx", scatter_dimension=1, tiled=True
        ).astype(jnp.float32),
        lax.psum_scatter(
            grad_value_all.astype(jnp.bfloat16), "ctx", scatter_dimension=1, tiled=True
        ).astype(jnp.float32),
    )
    grad_query = grad_query.reshape(row_count, head_cols)
    grad_key = grad_key.reshape(row_count, head_cols)
    grad_value = grad_value.reshape(row_count, head_cols)
    grad_prod_low = jnp.stack([grad_query, grad_key, grad_value], axis=1).astype(jnp.bfloat16)
    grad_qkv = jnp.einsum(
        "td,tcf->dcf", stream_low, grad_prod_low, preferred_element_type=jnp.float32
    )
    qkv_part = jnp.einsum(
        "tcf,dcf->td", grad_prod_low, back_qkv, preferred_element_type=jnp.float32
    )
    qv_term = jnp.stack([jnp.sum(grad_query, axis=0), jnp.sum(grad_value, axis=0)])
    up_term = jnp.sum(grad_pre, axis=0)
    gain_term = jnp.stack([gain_first, gain_second])
    shift_term = jnp.stack([shift_first, shift_second])
    bias_term = jnp.stack([jnp.sum(grad_first, axis=0), jnp.sum(grad_second, axis=0)])
    input_grad = across_heads(qkv_part) + grad_first
    qv_sum, up_sum, gain_sum, shift_sum, bias_sum = lax.psum(
        (qv_term, up_term, gain_term, shift_term, bias_term), ("shard", "ctx")
    )
    shares = (
        lax.psum_scatter(
            grad_qkv.astype(jnp.bfloat16), "shard", scatter_dimension=0, tiled=True
        ).astype(jnp.float32),
        lax.psum_scatter(
            grad_out.astype(jnp.bfloat16), "shard", scatter_dimension=1, tiled=True
        ).astype(jnp.float32),
        lax.psum_scatter(
            grad_up.astype(jnp.bfloat16), "shard", scatter_dimension=0, tiled=True
        ).astype(jnp.float32),
        lax.psum_scatter(
            grad_down.astype(jnp.bfloat16), "shard", scatter_dimension=1, tiled=True
        ).astype(jnp.float32),
    )
    qkv_share, out_share, up_share, down_share = (
        lax.psum(shares[0].astype(jnp.bfloat16), "ctx").astype(jnp.float32),
        lax.psum(shares[1].astype(jnp.bfloat16), "ctx").astype(jnp.float32),
        lax.psum(shares[2].astype(jnp.bfloat16), "ctx").astype(jnp.float32),
        lax.psum(shares[3].astype(jnp.bfloat16), "ctx").astype(jnp.float32),
    )
    return (
        layer_rows.reshape(seq_count, half_len, model_width),
        input_grad.reshape(seq_count, half_len, model_width),
        qkv_share,
        out_share,
        up_share,
        down_share,
        qv_sum,
        up_sum,
        gain_sum,
        shift_sum,
        bias_sum,
    )


def solution(mesh):
    placed = (
        P("shard", "ctx", None),
        P("shard", None),
        P("shard", None),
        P("shard", None, "tp"),
        P("tp", "shard"),
        P("shard", "tp"),
        P("tp", "shard"),
        P(None, "tp"),
        P("tp"),
        P(),
        P(),
        P(),
        P("shard", "ctx", None),
    )
    return jax.shard_map(
        shards,
        mesh=mesh,
        in_specs=placed,
        out_specs=(
            P("shard", "ctx", None),
            P("shard", "ctx", None),
            P("shard", None, "tp"),
            P("tp", "shard"),
            P("shard", "tp"),
            P("tp", "shard"),
            P(None, "tp"),
            P("tp"),
            P(),
            P(),
            P(),
        ),
        check_vma=False,
    )
```

profile of v0, /device:TPU:0, one launch (start us, length us, event | category | flops | bytes accessed | tf_op | source)
XLA Modules:
  0.0 712.3 jit_solution(5007047133472476936)
XLA Ops:
  8.9 25.9 %all_gather.22 = bf16[768,3,192]{2,0,1:T(8,128)(2,1)S(1)} all-gather(bf16[192,3,192]{2,0,1:T(8,128)(2,1)} %param.20), channel_id=1, replica_groups=mesh['shard'=4,'ctx'=2,'tp'=4] {'shard'}, dimensions={0}, use_global_device_ids=true | all-gather | bytes 1105920 | tf_op jit(solution)/shard_map/all_gather | solution.py:21
  40.2 14.4 %all_gather.25 = bf16[192,768]{0,1:T(8,128)(2,1)S(1)} all-gather(bf16[192,192]{0,1:T(8,128)(2,1)S(1)} %copy.47), channel_id=1, replica_groups=mesh['shard'=4,'ctx'=2,'tp'=4] {'shard'}, dimensions={1}, use_global_device_ids=true | all-gather | bytes 368640 | tf_op jit(solution)/shard_map/all_gather | solution.py:22
  63.5 14.4 %while.28 = (s32[]{:T(128)}, bf16[2,512,192]{1,2,0:T(8,128)(2,1)}, f32[2,3,512]{2,1,0:T(4,128)}, bf16[2,1024,192]{1,2,0:T(8,128)(2,1)S(1)}, s32[2,512]{1,0:T(2,1...) while((s32[]{:T(128)}, bf16[2,512,192]{1,2,0:T(8,128)(2,1)}, ...), condition=%wide.region_3.4_spmd.clone, body=%wide.region_0.3_spmd.sunk.clone | while | flops 422050304 | bytes 27828452 | solution.py:140
  85.1 84.7 %all-reduce.8.cloned.1.call-done = f32[1024,768]{1,0:T(8,128)} async-done(((f32[1024,768]{1,0:T(8,128)}), f32[1024,768]{1,0:T(8,128)}) %all-reduce.8.cloned.1.call-update) | async-done | bytes 3145744 | tf_op jit(solution)/shard_map/psum | solution.py:29
  169.7 3.3 fusion.42
  174.7 11.4 %multiply_convert_fusion.1 = (bf16[1024,768]{1,0:T(8,128)(2,1)}, f32[1024,768]{1,0:T(8,128)}, f32[1024,768]{1,0:T(8,128)}) fusion(f32[768]{0:T(1024)} %param.25, bf16[768,768]{1,0:T(8,128)(2,1)} %all-gather.3.cloned.1.call-done, f32[1024,768]{1,0:T(8,128)S(1)} %get-tuple-element.219, f32[768]{0:T(1024)} %get-tuple-element.159, f32[768]{0:T(1024)} %get-tuple-element.157, ...), kind=kOutput, calls=%fused_computation.56 | convolution fusion | flops 1263796224 | bytes 12207104 | tf_op jit(solution)/shard_map/dot_general | solution.py:150
  186.1 4.8 fusion.51
  191.0 87.1 %all-reduce.10.cloned.1.call-done = f32[1024,768]{1,0:T(8,128)} async-done(((f32[1024,768]{1,0:T(8,128)}), f32[1024,768]{1,0:T(8,128)}) %all-reduce.10.cloned.1.call-update) | async-done | bytes 3145744 | tf_op jit(solution)/shard_map/psum | solution.py:29
  289.7 3.2 fusion.46
  297.4 86.9 %all-reduce.12.cloned.1.call-done = f32[1024,768]{1,0:T(8,128)} async-done(((f32[1024,768]{1,0:T(8,128)}), f32[1024,768]{1,0:T(8,128)}) %all-reduce.12.cloned.1.call-update) | async-done | bytes 3145744 | tf_op jit(solution)/shard_map/psum | solution.py:29
  384.3 5.0 multiply_reduce_fusion.1
  394.1 30.5 %while.29 = (s32[]{:T(128)}, f32[2,512,192]{1,2,0:T(8,128)}, bf16[2,1024,192]{1,2,0:T(8,128)(2,1)}, bf16[2,1024,192]{1,2,0:T(8,128)(2,1)}, bf16[2,1024,192]{1,2,...) while((s32[]{:T(128)}, f32[2,512,192]{1,2,0:T(8,128)}, ...), condition=%wide.region_17.18_spmd.clone, body=%wide.region_15.17_spmd.sunk.clone | while | flops 1031240192 | bytes 76083512 | solution.py:176
  429.2 5.2 convolution_convert_fusion
  434.5 4.2 convolution_convert_fusion.1
  448.1 3.8 fusion.24
  452.0 17.1 %reduce-scatter.19.cloned.1.call-done = bf16[192,192]{1,0:T(8,128)(2,1)} async-done(((bf16[768,192]{1,0:T(8,128)(2,1)}), bf16[192,192]{1,0:T(8,128)(2,1)}) %reduce-scatter.19.cloned.1.call-update) | async-done | bytes 73744
  470.7 28.3 %reduce-scatter.17.cloned.1.call-done = bf16[768,192]{0,1:T(8,128)(2,1)} async-done(((bf16[768,768]{0,1:T(8,128)(2,1)}), bf16[768,192]{0,1:T(8,128)(2,1)}) %reduce-scatter.17.cloned.1.call-update) | async-done | bytes 294928 | tf_op jit(solution)/shard_map/reduce_scatter | solution.py:217
  499.0 30.1 %reduce-scatter.15.cloned.1.call-done = bf16[192,768]{1,0:T(8,128)(2,1)} async-done(((bf16[768,768]{1,0:T(8,128)(2,1)}), bf16[192,768]{1,0:T(8,128)(2,1)}) %reduce-scatter.15.cloned.1.call-update) | async-done | bytes 294928 | tf_op jit(solution)/shard_map/reduce_scatter | solution.py:214
  529.1 30.6 %reduce-scatter.13.cloned.1.call-done = bf16[192,3,192]{2,0,1:T(8,128)(2,1)} async-done(((bf16[768,3,192]{2,0,1:T(8,128)(2,1)}), bf16[192,3,192]{2,0,1:T(8,128)(2,1)}) %reduce-scatter.13.cloned.1.call-update) | async-done | bytes 221200 | tf_op jit(solution)/shard_map/reduce_scatter | solution.py:208
  559.8 4.4 convolution_bitcast_fusion
  568.3 12.1 %all-reduce.16.cloned.1.call-done = (bf16[192,3,192]{2,0,1:T(8,128)(2,1)}, bf16[192,192]{1,0:T(8,128)(2,1)}, bf16[192,768]{1,0:T(8,128)(2,1)}, bf16[768,192]{0,1:T(8,128)(2,1)}) async-done(((bf16[192,3,192]{2,0,1:T(8,128)(2,1)}, bf16[192,192]{1,0:T(8,128)(2,1)}, bf16[192,768]{1,0:T(8,128)(2,1)}, bf16[768,192]{0,1:T(8,128)(2,1)}), (bf16[192,3,192]{2,0,1:T(8,128)(2,1)}, bf16[192,192]{1,0:T(8,128)(2,1)}, ...) | async-done | bytes 884752 | tf_op jit(solution)/shard_map/psum | solution.py:222
  587.5 84.6 %all-reduce.14.cloned.1.call-done = f32[1024,768]{1,0:T(8,128)} async-done(((f32[1024,768]{1,0:T(8,128)}), f32[1024,768]{1,0:T(8,128)}) %all-reduce.14.cloned.1.call-update) | async-done | bytes 3145744 | tf_op jit(solution)/shard_map/psum | solution.py:29
  672.1 4.0 add_reduce_fusion
  676.1 28.9 %all-reduce = (f32[2,192]{1,0:T(2,128)}, f32[768]{0:T(1024)}, f32[2,768]{1,0:T(2,128)}, f32[2,768]{1,0:T(2,128)}, f32[2,768]{1,0:T(2,128)}) all-reduce(f32[2,192]{1,0:T(2,128)S(1)} %pad_maximum_fusion.3, f32[768]{0:T(1024)S(1)} %copy-done.48, ...), channel_id=1, replica_groups=mesh['shard'=4,'ctx'=2,'tp'=4] {'shard','ctx'}, use_global_device_ids=true, to_apply=%region_31.32 | all-reduce | flops 5760 | bytes 46080 | tf_op jit(solution)/shard_map/psum | solution.py:204
  (286 shorter events, 115.8 us)
Async XLA Ops:
  8.0 28.1 %copy-start.44 = (f32[2,768]{1,0:T(2,128)S(1)}, f32[2,768]{1,0:T(2,128)}, u32[]{:S(2)}) copy-start(f32[2,768]{1,0:T(2,128)} %param.18) | copy-start | bytes 18436
  8.0 28.1 %copy-start.14 = (bf16[2,512,768]{2,1,0:T(8,128)(2,1)S(1)}, bf16[2,512,768]{2,1,0:T(8,128)(2,1)}, u32[]{:S(2)}) copy-start(bf16[2,512,768]{2,1,0:T(8,128)(2,1)} %param.17) | copy-start | bytes 4718596
  8.0 161.7 %all-reduce.8.cloned.1.call-start = ((), (), s32[]{:S(2)}) async-start(), calls=%async_computation.6 | async-start | bytes 6291456 | tf_op jit(solution)/shard_map/psum | solution.py:29
  54.6 24.5 %copy-start.9 = (bf16[192,768]{0,1:T(8,128)(2,1)}, bf16[192,768]{0,1:T(8,128)(2,1)S(1)}, u32[]{:S(2)}) copy-start(bf16[192,768]{0,1:T(8,128)(2,1)S(1)} %all_gather.25) | copy-start | bytes 884740
  56.5 5.7 copy-start.23
  81.5 93.2 %all-gather.3.cloned.1.call-start = ((), (), s32[]{:S(2)}) async-start(), calls=%async_computation.7 | async-start | bytes 1474560 | tf_op jit(solution)/shard_map/all_gather | solution.py:23
  82.1 104.0 %all-gather.5.cloned.1.call-start = ((), (), s32[]{:S(2)}) async-start(), calls=%async_computation.8 | async-start | bytes 1474560 | tf_op jit(solution)/shard_map/all_gather | solution.py:24
  82.7 195.4 %all-reduce.10.cloned.1.call-start = ((), (), s32[]{:S(2)}) async-start(), calls=%async_computation.9 | async-start | bytes 6291456 | tf_op jit(solution)/shard_map/psum | solution.py:29
  191.0 193.3 %all-reduce.12.cloned.1.call-start = ((), (), s32[]{:S(2)}) async-start(), calls=%async_computation.10 | async-start | bytes 6291456 | tf_op jit(solution)/shard_map/psum | solution.py:29
  287.0 5.8 copy-start.5
  287.0 5.8 copy-start.42
  297.2 145.9 %reduce-scatter.9.cloned.1.call-start = ((), (), s32[]{:S(2)}) async-start(), calls=%async_computation.11 | async-start | bytes 1179648 | tf_op jit(solution)/shard_map/reduce_scatter | solution.py:181
  424.6 20.2 %reduce-scatter.11.cloned.1.call-start = ((), (), s32[]{:S(2)}) async-start(), calls=%async_computation.12 | async-start | bytes 1179648 | tf_op jit(solution)/shard_map/reduce_scatter | solution.py:184
  425.3 43.8 %reduce-scatter.19.cloned.1.call-start = ((), (), s32[]{:S(2)}) async-start(), calls=%async_computation.17 | async-start | bytes 491520
  428.9 70.1 %reduce-scatter.17.cloned.1.call-start = ((), (), s32[]{:S(2)}) async-start(), calls=%async_computation.16 | async-start | bytes 1474560 | tf_op jit(solution)/shard_map/reduce_scatter | solution.py:217
  434.4 94.7 %reduce-scatter.15.cloned.1.call-start = ((), (), s32[]{:S(2)}) async-start(), calls=%async_computation.15 | async-start | bytes 1474560 | tf_op jit(solution)/shard_map/reduce_scatter | solution.py:214
  438.8 120.9 %reduce-scatter.13.cloned.1.call-start = ((), (), s32[]{:S(2)}) async-start(), calls=%async_computation.14 | async-start | bytes 1474560 | tf_op jit(solution)/shard_map/reduce_scatter | solution.py:208
  448.1 111.7 %copy-start.7 = (bf16[768,3,192]{2,0,1:T(8,128)(2,1)S(1)}, bf16[768,3,192]{2,0,1:T(8,128)(2,1)}, u32[]{:S(2)}) copy-start(bf16[768,3,192]{2,0,1:T(8,128)(2,1)} %copy-done.6) | copy-start | bytes 2654212
  451.9 128.5 %all-reduce.16.cloned.1.call-start = ((), (), s32[]{:S(2)}) async-start(), calls=%async_computation.18 | async-start | bytes 1966080 | tf_op jit(solution)/shard_map/psum | solution.py:222
  559.8 112.3 %all-reduce.14.cloned.1.call-start = ((), (), s32[]{:S(2)}) async-start(), calls=%async_computation.13 | async-start | bytes 6291456 | tf_op jit(solution)/shard_map/psum | solution.py:29
  564.3 107.8 %copy-start.1 = (f32[1024,768]{1,0:T(8,128)S(1)}, f32[1024,768]{1,0:T(8,128)}, u32[]{:S(2)}) copy-start(f32[1024,768]{1,0:T(8,128)} %copy-done) | copy-start | bytes 9437188
  564.3 107.8 %copy-start.30 = (f32[1024]{0:T(1024)S(1)}, f32[1024]{0:T(1024)}, u32[]{:S(2)}) copy-start(f32[1024]{0:T(1024)} %copy-done.29) | copy-start | bytes 12292
  587.5 88.6 %copy-start.36 = (f32[2,768]{1,0:T(2,128)S(1)}, f32[2,768]{1,0:T(2,128)}, u32[]{:S(2)}) copy-start(f32[2,768]{1,0:T(2,128)} %get-tuple-element.244) | copy-start | bytes 18436
  587.5 88.6 %copy-start.48 = (f32[768]{0:T(1024)S(1)}, f32[768]{0:T(1024)}, u32[]{:S(2)}) copy-start(f32[768]{0:T(1024)} %get-tuple-element.241) | copy-start | bytes 9220
  (55 other events, 141.2 us)
Sparse Core Ops, SparseCore 0:
  81.6 88.0 all-reduce.7
  191.1 86.9 all-reduce.9
  297.3 86.9 all-reduce.11
Sparse Core Ops, SparseCore 1:
  83.6 31.2 all-gather.2
  116.2 29.3 all-gather.4
  424.7 8.1 reduce-scatter.8
  435.1 9.2 reduce-scatter.10
  447.2 21.8 reduce-scatter.18
  471.4 27.5 reduce-scatter.16
  501.2 27.8 reduce-scatter.14
  531.9 27.8 reduce-scatter.12
  562.7 17.6 all-reduce.15
  584.1 87.9 all-reduce.13
where the time goes:
time: 720 us; the launch traced here: 712 us
  waiting for transfers between devices  463 us (64%)
  blocking collectives  73.9 us (10%)
  matrix products  68.3 us (9%)
  other arithmetic  48.8 us (7%)
  local copies, waits for them, and re-layouts  39.9 us (6%)
  between operations  16.2 us (2%)
    psum x4, waiting for transfers between devices, across_heads(): return lax.psum(term_rows, 'tp')  343 us
    reduce_scatter x1, waiting for transfers between devices, shards(): lax.psum_scatter(grad_qkv.astype(jnp.bfloat16), 'shard', scatter_dimensio...  30.6 us
    reduce_scatter x1, waiting for transfers between devices, shards(): lax.psum_scatter(grad_up.astype(jnp.bfloat16), 'shard', scatter_dimension...  30.1 us
    psum x1, blocking collectives, shards(): lax.psum((qv_term, up_term, gain_term, shift_term, bias_term), ('shard',...  28.9 us
    reduce_scatter x1, waiting for transfers between devices, shards(): lax.psum_scatter(grad_down.astype(jnp.bfloat16), 'shard', scatter_dimensi...  28.3 us
    all_gather x1, blocking collectives, fetch_weights(): lax.all_gather(w_qkv, 'shard', axis=0, tiled=True)  25.9 us
    unnamed x14, waiting for transfers between devices  19 us
    all_gather x1, blocking collectives, fetch_weights(): lax.all_gather(w_out, 'shard', axis=1, tiled=True)  14.4 us
  transfers between devices with their start and end apart: 13, of which 9 were waited for; matrix products, arithmetic and copies ran while one was open for 9% of the time, Pallas kernels for 0%

commit v1 on v0

--- a/solution.py
+++ b/solution.py
@@ -26,7 +26,7 @@
 
 
 def across_heads(term_rows):
-    return lax.psum(term_rows, "tp")
+    return jnp.sum(lax.all_gather(term_rows, "tp"), axis=0)
 
 
 def masked_scores(query_blk, key_blk, labels_query, labels_key):

time: 720 us -> 933 us (1.30)
  waiting for transfers between devices: 463 us -> 642 us
  other arithmetic: 48.8 us -> 82.2 us
    all_gather x0 -> x4, waiting for transfers between devices: none -> 483 us  [across_heads(): return jnp.sum(lax.all_gather(term_rows, 'tp'), axis=0)]
    psum x4 -> x0, waiting for transfers between devices: 343 us -> none  [across_heads(): return lax.psum(term_rows, 'tp')]
    reduce_sum x0 -> x5, other arithmetic: none -> 38.1 us  [the longest x4 30.1 us: across_heads(): return jnp.sum(lax.all_gather(term_rows, 'tp'), axis=0)]
    all_gather x1, waiting for transfers between devices: 0.01 us -> 19.6 us  [fetch_weights(): lax.all_gather(w_down, 'shard', axis=1, tiled=True)]
    all_gather x1, waiting for transfers between devices: 0.01 us -> 15.6 us  [fetch_weights(): lax.all_gather(w_up, 'shard', axis=0, tiled=True)]
  transfers between devices with their start and end apart: 13 -> 13, of which waited for: 9 -> 11; matrix products, arithmetic and copies ran while one was open for 9% -> 7% of each run, Pallas kernels for 0% -> 0%
where the time goes in v1:
time: 933 us; the launch traced here: 925 us
  waiting for transfers between devices  642 us (69%)
  other arithmetic  82.2 us (9%)
  blocking collectives  74.1 us (8%)
  matrix products  68.5 us (7%)
  local copies, waits for them, and re-layouts  41.2 us (4%)
  between operations  14.9 us (2%)
    all_gather x4, waiting for transfers between devices, across_heads(): return jnp.sum(lax.all_gather(term_rows, 'tp'), axis=0)  483 us
    reduce_scatter x1, waiting for transfers between devices, shards(): lax.psum_scatter(grad_qkv.astype(jnp.bfloat16), 'shard', scatter_dimensio...  30.9 us
    reduce_scatter x1, waiting for transfers between devices, shards(): lax.psum_scatter(grad_up.astype(jnp.bfloat16), 'shard', scatter_dimension...  30.1 us
    reduce_sum x4, other arithmetic, across_heads(): return jnp.sum(lax.all_gather(term_rows, 'tp'), axis=0)  30.1 us
    psum x1, blocking collectives, shards(): lax.psum((qv_term, up_term, gain_term, shift_term, bias_term), ('shard',...  29 us
    reduce_scatter x1, waiting for transfers between devices, shards(): lax.psum_scatter(grad_down.astype(jnp.bfloat16), 'shard', scatter_dimensi...  28.3 us
    all_gather x1, blocking collectives, fetch_weights(): lax.all_gather(w_qkv, 'shard', axis=0, tiled=True)  26 us
    unnamed x14, waiting for transfers between devices  19.6 us
  transfers between devices with their start and end apart: 13, of which 11 were waited for; matrix products, arithmetic and copies ran while one was open for 7% of the time, Pallas kernels for 0%

profile of v1, /device:TPU:0, one launch (start us, length us, event | category | flops | bytes accessed | tf_op | source)
XLA Modules:
  0.0 925.0 jit_solution(1125531877590279072)
XLA Ops:
  7.3 26.0 %all_gather.46 = bf16[768,3,192]{2,0,1:T(8,128)(2,1)S(1)} all-gather(bf16[192,3,192]{2,0,1:T(8,128)(2,1)} %param.20), channel_id=1, replica_groups=mesh['shard'=4,'ctx'=2,'tp'=4] {'shard'}, dimensions={0}, use_global_device_ids=true | all-gather | bytes 1105920 | tf_op jit(solution)/shard_map/all_gather | solution.py:21
  38.8 14.4 %all_gather.49 = bf16[192,768]{0,1:T(8,128)(2,1)S(1)} all-gather(bf16[192,192]{0,1:T(8,128)(2,1)S(1)} %copy.47), channel_id=1, replica_groups=mesh['shard'=4,'ctx'=2,'tp'=4] {'shard'}, dimensions={1}, use_global_device_ids=true | all-gather | bytes 368640 | tf_op jit(solution)/shard_map/all_gather | solution.py:22
  64.1 12.8 %while.28 = (s32[]{:T(128)}, bf16[2,512,192]{1,2,0:T(8,128)(2,1)S(1)}, f32[2,3,512]{2,1,0:T(4,128)}, bf16[2,1024,192]{1,2,0:T(8,128)(2,1)S(1)}, s32[2,512]{1,0:T...) while((s32[]{:T(128)}, ...), condition=%wide.region_3.4_spmd.clone, body=%wide.region_0.3_spmd.sunk.clone | while | flops 422050304 | bytes 24580212 | solution.py:140
  83.0 120.1 %all-gather.15.cloned.1.call-done = f32[4096,768]{1,0:T(8,128)} async-done(((f32[1024,768]{1,0:T(8,128)}), f32[4096,768]{1,0:T(8,128)}) %all-gather.15.cloned.1.call-update) | async-done | bytes 12582928 | tf_op jit(solution)/shard_map/all_gather | solution.py:29
  203.1 7.5 reduce_sum.251
  219.3 15.6 %all-gather.11.cloned.1.call-done = bf16[768,768]{1,0:T(8,128)(2,1)} async-done(((bf16[192,768]{1,0:T(8,128)(2,1)}), bf16[768,768]{1,0:T(8,128)(2,1)}) %all-gather.11.cloned.1.call-update) | async-done | bytes 1179664 | tf_op jit(solution)/shard_map/all_gather | solution.py:23
  234.9 11.6 %multiply_convert_fusion.1 = (bf16[1024,768]{1,0:T(8,128)(2,1)}, f32[1024,768]{1,0:T(8,128)}, f32[1024,768]{1,0:T(8,128)}) fusion(f32[768]{0:T(1024)} %param.25, bf16[768,768]{1,0:T(8,128)(2,1)} %all-gather.11.cloned.1.call-done, f32[1024,768]{1,0:T(8,128)} %add_subtract_fusion, f32[768]{0:T(1024)} %get-tuple-element.162, f32[768]{0:T(1024)S(1)} %get-tuple-element.160, ...), kind=kOutput, calls=%fused_computation.56 | convolution fusion | flops 1263009792 | bytes 12203008 | tf_op jit(solution)/shard_map/dot_general | solution.py:150
  246.5 19.6 %all-gather.13.cloned.1.call-done = bf16[768,768]{0,1:T(8,128)(2,1)} async-done(((bf16[768,192]{0,1:T(8,128)(2,1)}), bf16[768,768]{0,1:T(8,128)(2,1)}) %all-gather.13.cloned.1.call-update) | async-done | bytes 1179664 | tf_op jit(solution)/shard_map/all_gather | solution.py:24
  271.1 121.5 %all-gather.17.cloned.1.call-done = f32[4096,768]{1,0:T(8,128)} async-done(((f32[1024,768]{1,0:T(8,128)}), f32[4096,768]{1,0:T(8,128)}) %all-gather.17.cloned.1.call-update) | async-done | bytes 12582928 | tf_op jit(solution)/shard_map/all_gather | solution.py:29
  392.6 7.5 reduce_sum.255
  419.2 122.1 %all-gather.19.cloned.1.call-done = f32[4096,768]{1,0:T(8,128)} async-done(((f32[1024,768]{1,0:T(8,128)}), f32[4096,768]{1,0:T(8,128)}) %all-gather.19.cloned.1.call-update) | async-done | bytes 12582928 | tf_op jit(solution)/shard_map/all_gather | solution.py:29
  541.2 7.5 reduce_sum.262
  548.7 8.1 add_reduce_fusion
  564.2 30.7 %while.29 = (s32[]{:T(128)}, f32[2,512,192]{1,2,0:T(8,128)}, bf16[2,1024,192]{1,2,0:T(8,128)(2,1)}, bf16[2,1024,192]{1,2,0:T(8,128)(2,1)}, bf16[2,1024,192]{1,2,...) while((s32[]{:T(128)}, f32[2,512,192]{1,2,0:T(8,128)}, ...), condition=%wide.region_17.18_spmd.clone, body=%wide.region_15.17_spmd.sunk.clone | while | flops 1031240192 | bytes 76083512 | solution.py:176
  598.5 4.8 convolution_convert_fusion
  603.5 5.1 convolution_convert_fusion.1
  622.2 17.4 %reduce-scatter.19.cloned.1.call-done = bf16[192,192]{1,0:T(8,128)(2,1)} async-done(((bf16[768,192]{1,0:T(8,128)(2,1)}), bf16[192,192]{1,0:T(8,128)(2,1)}) %reduce-scatter.19.cloned.1.call-update) | async-done | bytes 73744
  641.2 28.3 %reduce-scatter.17.cloned.1.call-done = bf16[768,192]{0,1:T(8,128)(2,1)} async-done(((bf16[768,768]{0,1:T(8,128)(2,1)}), bf16[768,192]{0,1:T(8,128)(2,1)}) %reduce-scatter.17.cloned.1.call-update) | async-done | bytes 294928 | tf_op jit(solution)/shard_map/reduce_scatter | solution.py:217
  669.5 30.1 %reduce-scatter.15.cloned.1.call-done = bf16[192,768]{1,0:T(8,128)(2,1)} async-done(((bf16[768,768]{1,0:T(8,128)(2,1)}), bf16[192,768]{1,0:T(8,128)(2,1)}) %reduce-scatter.15.cloned.1.call-update) | async-done | bytes 294928 | tf_op jit(solution)/shard_map/reduce_scatter | solution.py:214
  699.6 30.9 %reduce-scatter.13.cloned.1.call-done = bf16[192,3,192]{2,0,1:T(8,128)(2,1)} async-done(((bf16[768,3,192]{2,0,1:T(8,128)(2,1)}), bf16[192,3,192]{2,0,1:T(8,128)(2,1)}) %reduce-scatter.13.cloned.1.call-update) | async-done | bytes 221200 | tf_op jit(solution)/shard_map/reduce_scatter | solution.py:208
  736.1 15.5 %all-reduce.4.cloned.1.call-done = (bf16[192,3,192]{2,0,1:T(8,128)(2,1)}, bf16[192,192]{1,0:T(8,128)(2,1)}, bf16[192,768]{1,0:T(8,128)(2,1)}, bf16[768,192]{0,1:T(8,128)(2,1)}) async-done(((bf16[192,3,192]{2,0,1:T(8,128)(2,1)}, bf16[192,192]{1,0:T(8,128)(2,1)}, bf16[192,768]{1,0:T(8,128)(2,1)}, bf16[768,192]{0,1:T(8,128)(2,1)}), (bf16[192,3,192]{2,0,1:T(8,128)(2,1)}, bf16[192,192]{1,0:T(8,128)(2,1)}, ...) | async-done | bytes 884752 | tf_op jit(solution)/shard_map/psum | solution.py:222
  758.6 119.0 %all-gather.21.cloned.1.call-done = f32[4096,768]{1,0:T(8,128)} async-done(((f32[1024,768]{1,0:T(8,128)}), f32[4096,768]{1,0:T(8,128)}) %all-gather.21.cloned.1.call-update) | async-done | bytes 12582928 | tf_op jit(solution)/shard_map/all_gather | solution.py:29
  877.7 7.6 reduce_sum.267
  889.3 29.0 %all-reduce = (f32[2,192]{1,0:T(2,128)}, f32[768]{0:T(1024)}, f32[2,768]{1,0:T(2,128)}, f32[2,768]{1,0:T(2,128)}, f32[2,768]{1,0:T(2,128)}) all-reduce(f32[2,192]{1,0:T(2,128)S(1)} %pad_maximum_fusion.3, f32[768]{0:T(1024)S(1)} %copy-done.60, ...), channel_id=1, replica_groups=mesh['shard'=4,'ctx'=2,'tp'=4] {'shard','ctx'}, use_global_device_ids=true, to_apply=%region_31.32 | all-reduce | flops 5760 | bytes 46080 | tf_op jit(solution)/shard_map/psum | solution.py:204
  (316 shorter events, 140.6 us)
Async XLA Ops:
  7.2 27.5 %copy-start.51 = (f32[2,768]{1,0:T(2,128)S(1)}, f32[2,768]{1,0:T(2,128)}, u32[]{:S(2)}) copy-start(f32[2,768]{1,0:T(2,128)} %param.18) | copy-start | bytes 18436
  7.2 27.5 %copy-start.15 = (bf16[2,512,768]{2,1,0:T(8,128)(2,1)S(1)}, bf16[2,512,768]{2,1,0:T(8,128)(2,1)}, u32[]{:S(2)}) copy-start(bf16[2,512,768]{2,1,0:T(8,128)(2,1)} %param.17) | copy-start | bytes 4718596
  7.2 195.9 %all-gather.15.cloned.1.call-start = ((), (), s32[]{:S(2)}) async-start(), calls=%async_computation.13 | async-start | bytes 15728640 | tf_op jit(solution)/shard_map/all_gather | solution.py:29
  53.3 23.8 %copy-start.18 = (bf16[192,768]{0,1:T(8,128)(2,1)}, bf16[192,768]{0,1:T(8,128)(2,1)S(1)}, u32[]{:S(2)}) copy-start(bf16[192,768]{0,1:T(8,128)(2,1)S(1)} %all_gather.49) | copy-start | bytes 884740
  55.1 7.7 copy-start.30
  79.4 155.5 %all-gather.11.cloned.1.call-start = ((), (), s32[]{:S(2)}) async-start(), calls=%async_computation.6 | async-start | bytes 1474560 | tf_op jit(solution)/shard_map/all_gather | solution.py:23
  80.2 185.9 %all-gather.13.cloned.1.call-start = ((), (), s32[]{:S(2)}) async-start(), calls=%async_computation.7 | async-start | bytes 1474560 | tf_op jit(solution)/shard_map/all_gather | solution.py:24
  80.9 311.7 %all-gather.17.cloned.1.call-start = ((), (), s32[]{:S(2)}) async-start(), calls=%async_computation.14 | async-start | bytes 15728640 | tf_op jit(solution)/shard_map/all_gather | solution.py:29
  270.9 270.4 %all-gather.19.cloned.1.call-start = ((), (), s32[]{:S(2)}) async-start(), calls=%async_computation.15 | async-start | bytes 15728640 | tf_op jit(solution)/shard_map/all_gather | solution.py:29
  418.7 194.7 %reduce-scatter.9.cloned.1.call-start = ((), (), s32[]{:S(2)}) async-start(), calls=%async_computation.8 | async-start | bytes 1179648 | tf_op jit(solution)/shard_map/reduce_scatter | solution.py:181
  548.7 8.1 copy-start.46
  548.7 8.1 copy-start.48
  548.7 8.1 copy-start.33
  548.7 8.2 copy-start.35
  548.7 11.1 %copy-start.19 = (bf16[192,768]{0,1:T(8,128)(2,1)S(1)}, bf16[192,768]{0,1:T(8,128)(2,1)}, u32[]{:S(2)}) copy-start(bf16[192,768]{0,1:T(8,128)(2,1)} %copy-done.18) | copy-start | bytes 884740
  564.2 31.7 %copy-start.4 = (f32[2,512,768]{2,1,0:T(8,128)S(1)}, f32[2,512,768]{2,1,0:T(8,128)}, u32[]{:S(2)}) copy-start(f32[2,512,768]{2,1,0:T(8,128)} %get-tuple-element.213) | copy-start | bytes 9437188
  594.9 20.2 %reduce-scatter.11.cloned.1.call-start = ((), (), s32[]{:S(2)}) async-start(), calls=%async_computation.9 | async-start | bytes 1179648 | tf_op jit(solution)/shard_map/reduce_scatter | solution.py:184
  595.6 43.9 %reduce-scatter.19.cloned.1.call-start = ((), (), s32[]{:S(2)}) async-start(), calls=%async_computation.17 | async-start | bytes 491520
  598.5 71.0 %reduce-scatter.17.cloned.1.call-start = ((), (), s32[]{:S(2)}) async-start(), calls=%async_computation.12 | async-start | bytes 1474560 | tf_op jit(solution)/shard_map/reduce_scatter | solution.py:217
  603.4 96.2 %reduce-scatter.15.cloned.1.call-start = ((), (), s32[]{:S(2)}) async-start(), calls=%async_computation.11 | async-start | bytes 1474560 | tf_op jit(solution)/shard_map/reduce_scatter | solution.py:214
  608.6 121.8 %reduce-scatter.13.cloned.1.call-start = ((), (), s32[]{:S(2)}) async-start(), calls=%async_computation.10 | async-start | bytes 1474560 | tf_op jit(solution)/shard_map/reduce_scatter | solution.py:208
  618.3 112.2 %copy-start.17 = (bf16[768,3,192]{2,0,1:T(8,128)(2,1)S(1)}, bf16[768,3,192]{2,0,1:T(8,128)(2,1)}, u32[]{:S(2)}) copy-start(bf16[768,3,192]{2,0,1:T(8,128)(2,1)} %copy-done.16) | copy-start | bytes 2654212
  622.1 129.5 %all-reduce.4.cloned.1.call-start = ((), (), s32[]{:S(2)}) async-start(), calls=%async_computation.18 | async-start | bytes 1966080 | tf_op jit(solution)/shard_map/psum | solution.py:222
  730.5 147.2 %all-gather.21.cloned.1.call-start = ((), (), s32[]{:S(2)}) async-start(), calls=%async_computation.16 | async-start | bytes 15728640 | tf_op jit(solution)/shard_map/all_gather | solution.py:29
  (63 other events, 171.2 us)
Sparse Core Ops, SparseCore 0:
  79.5 123.4 all-gather.14
  204.6 30.2 all-gather.10
  236.5 29.4 all-gather.12
  271.0 121.5 all-gather.16
  418.8 122.3 all-gather.18
  595.0 8.1 reduce-scatter.8
  605.4 9.2 reduce-scatter.10
  617.6 21.9 reduce-scatter.18
  641.9 27.5 reduce-scatter.16
  671.7 27.9 reduce-scatter.14
  702.5 27.9 reduce-scatter.12
  733.5 18.0 all-reduce.3
  754.0 123.6 all-gather.20
